TPU v7x, 32 devices: a whole 2x2x4 slice. The times are simulated.
32 devices in a mesh: segment: 4 (over y, x), vocab: 8 (over z, core).
Axes of the slice: x: 2, y: 2, z: 4, core: 2. Of those that a mesh axis runs over, the one named last changes fastest.
Arguments:
- trunk_out: bfloat16 [160, 7168], P(None, 'vocab'), may hold values from -12 to 12
- embeds: bfloat16 [164, 7168], P(None, 'vocab'), may hold values from -12 to 12
- token_ids: int32 [164], replicated, may hold values from 0 to 8191
- module_weight: bfloat16 [4, 2, 7168, 7168], P('segment', None, 'vocab'), may hold values from -0.046875 to 0.046875
- hidden_gain: bfloat16 [3, 7168], P(None, 'vocab'), may hold values from 0.25 to 1.75
- embed_gain: bfloat16 [3, 7168], P(None, 'vocab'), may hold values from 0.25 to 1.75
- out_gain: bfloat16 [4, 7168], P('segment'), may hold values from 0.25 to 1.75
- head_weight: bfloat16 [7168, 8192], P('segment', 'vocab'), may hold values from -0.21260502 to 0.21260502
Outputs:
- losses: float32 [4, 160], P('segment')
All inputs are finite; a program needn't handle non-finite values.
Results may differ from a plain program's by a relative error of at most 0.00095.
Values may be sent and summed in bfloat16 or wider, within the bound.
No kernel may reach another device: no remote copies, remote signals or barrier semaphores. Data moves between devices by JAX's collectives and lax.ppermute only.
A program may use at most 128 MiB of HBM per device.

v0:
```python
import jax
import jax.numpy as jnp
from jax import lax
from jax.sharding import PartitionSpec as P

D = 7168
TOK = 160
MICRO = 4
EPSILON = 1e-06


def passed_along(block, axis, distance):
    devices = range(lax.axis_size(axis))
    route = [(i - distance, i) for i in devices if i - distance in devices]
    return lax.ppermute(block, axis, route)


def combined_all(shard, axis, combine):
    everything = jax.tree.map(lambda part: lax.all_gather(part, axis), shard)
    first = jax.tree.map(lambda part: part[0], everything)

    def step(k, so_far):
        return combine(so_far, jax.tree.map(lambda part: part[k], everything))

    return lax.fori_loop(1, lax.axis_size(axis), step, first)


def merge_softmax(earlier, second):
    highest = jnp.maximum(earlier[0], second[0])
    summed = earlier[1] * jnp.exp(earlier[0] - highest) + second[1] * jnp.exp(second[0] - highest)
    return (highest, summed, earlier[2] + second[2])


def per_device(
    trunk_out, embeds, token_ids, module_weight, hidden_gain, embed_gain, out_gain, head_weight
):
    sections = lax.axis_size("segment")
    section = lax.axis_index("segment")
    shard_index = lax.axis_index("vocab")
    local_width = trunk_out.shape[1]
    micro_rows = TOK // MICRO
    vocab_width = head_weight.shape[1]
    depth_count = hidden_gain.shape[0]
    embed_float = embeds.astype(jnp.float32)
    embed_squares = lax.psum(jnp.sum(embed_float * embed_float, axis=1), "vocab")
    embed_scale = lax.rsqrt(embed_squares / D + EPSILON)
    module_index = jnp.maximum(section - 1, 0)
    module_block = module_weight[0]
    embed_scaling = lax.dynamic_index_in_dim(embed_gain, module_index, 0, keepdims=False).astype(
        jnp.float32
    )
    next_scaling = lax.dynamic_index_in_dim(
        hidden_gain, jnp.minimum(section, depth_count - 1), 0, keepdims=False
    ).astype(jnp.float32)
    out_scaling = out_gain[0].astype(jnp.float32)
    targets = lax.dynamic_slice_in_dim(token_ids, section + 1, TOK, 0) - shard_index * vocab_width
    whole_head = lax.all_gather(head_weight, "segment", axis=0, tiled=True)
    column_ids = lax.broadcasted_iota(jnp.int32, (micro_rows, vocab_width), 1)
    incoming = jnp.zeros((micro_rows, local_width), jnp.bfloat16)
    stored_tops = jnp.zeros((TOK,), jnp.float32)
    stored_totals = jnp.ones((TOK,), jnp.float32)
    stored_picks = jnp.zeros((TOK,), jnp.float32)
    for moment in range(MICRO + sections - 1):
        micro_index = moment - section
        active = (micro_index >= 0) & (micro_index < MICRO)
        first_row = jnp.clip(micro_index, 0, MICRO - 1) * micro_rows
        own_rows = lax.dynamic_slice_in_dim(trunk_out, first_row, micro_rows, 0)
        embed_rows = lax.dynamic_slice_in_dim(embed_float, first_row + section, micro_rows, 0)
        embed_factor = lax.dynamic_slice_in_dim(embed_scale, first_row + section, micro_rows, 0)
        embed_normed = (embed_rows * embed_factor[:, None] * embed_scaling).astype(jnp.bfloat16)
        partial_value = jnp.dot(incoming, module_block[0], preferred_element_type=jnp.float32)
        partial_value = partial_value + jnp.dot(
            embed_normed, module_block[1], preferred_element_type=jnp.float32
        )
        leading = section == 0
        placed = lax.dynamic_update_slice_in_dim(
            jnp.zeros((micro_rows, D), jnp.float32),
            own_rows.astype(jnp.float32),
            shard_index * local_width,
            1,
        )
        full_rows = lax.psum(jnp.where(leading, placed, partial_value), "vocab").astype(
            jnp.bfloat16
        )
        rows_float = full_rows.astype(jnp.float32)
        inverse_rms = lax.rsqrt(jnp.mean(rows_float * rows_float, axis=1, keepdims=True) + EPSILON)
        head_input = (rows_float * inverse_rms * out_scaling).astype(jnp.bfloat16)
        own_columns = lax.dynamic_slice_in_dim(
            rows_float, shard_index * local_width, local_width, 1
        )
        passed = (own_columns * inverse_rms * next_scaling).astype(jnp.bfloat16)
        incoming = passed_along(passed, "segment", 1)
        logits = jnp.dot(head_input, whole_head, preferred_element_type=jnp.float32)
        row_targets = lax.dynamic_slice_in_dim(targets, first_row, micro_rows, 0)
        row_target = jnp.sum(jnp.where(column_ids == row_targets[:, None], logits, 0.0), axis=1)
        row_top = jnp.max(logits, axis=1)
        row_total = jnp.sum(jnp.exp(logits - row_top[:, None]), axis=1)
        stored_tops = jnp.where(
            active, lax.dynamic_update_slice_in_dim(stored_tops, row_top, first_row, 0), stored_tops
        )
        stored_totals = jnp.where(
            active,
            lax.dynamic_update_slice_in_dim(stored_totals, row_total, first_row, 0),
            stored_totals,
        )
        stored_picks = jnp.where(
            active,
            lax.dynamic_update_slice_in_dim(stored_picks, row_target, first_row, 0),
            stored_picks,
        )
    merged_tops, merged_totals, merged_picks = combined_all(
        (stored_tops, stored_totals, stored_picks), "vocab", merge_softmax
    )
    losses = merged_tops + jnp.log(merged_totals) - merged_picks
    return losses[None, :]


def solution(mesh):
    in_specs = (
        P(None, "vocab"),
        P(None, "vocab"),
        P(),
        P("segment", None, "vocab", None),
        P(None, "vocab"),
        P(None, "vocab"),
        P("segment", None),
        P("segment", "vocab"),
    )
    out_specs = P("segment", None)
    return jax.shard_map(
        per_device, mesh=mesh, in_specs=in_specs, out_specs=out_specs, check_vma=False
    )
```

profile of v0, /device:TPU:5, one launch (start us, length us, event | category | flops | bytes accessed | tf_op | source)
XLA Modules:
  0.0 643.8 jit_solution(13789716217223740814)
XLA Ops:
  7.7 13.8 %psum.56 = f32[164]{0:T(256)S(1)} all-reduce(f32[164]{0:T(256)S(1)} %multiply_reduce_fusion.6), channel_id=1, replica_groups=mesh['segment'=4,'vocab'=8] {'vocab'}, use_global_device_ids=true, to_apply=%region_1.0 | all-reduce | flops 164 | bytes 1312 | tf_op jit(solution)/shard_map/psum | solution.py:45
  21.6 7.5 %fusion.12 = f32[40,7168]{1,0:T(8,128)S(1)} fusion(bf16[1,2,896,7168]{3,2,1,0:T(8,128)(2,1)} %param.13, f32[164,896]{1,0:T(8,128)S(1)} %convert_element_type.133, s32[]{:T(128)S(6)} %select_n.352, f32[896]{0:T(1024)S(1)} %fusion.139, f32[40]{0:T(128)S(1)} %get-tuple-element.231), kind=kOutput, calls=%fused_computation.16 | convolution fusion | flops 513909760 | bytes 14139908 | tf_op jit(solution)/shard_map/dot_general | solution.py:72
  30.1 5.9 fusion.67
  36.1 56.9 %all-reduce.7 = bf16[40,7168]{1,0:T(8,128)(2,1)S(1)} all-reduce(f32[40,7168]{1,0:T(8,128)S(1)} %fusion.67), channel_id=1, replica_groups=mesh['segment'=4,'vocab'=8] {'vocab'}, use_global_device_ids=true, to_apply=%region_2.3 | all-reduce | flops 286720 | bytes 1720320 | tf_op jit(solution)/shard_map/psum | solution.py:82
  94.0 3.3 collective-permute-start
  99.6 8.2 %fusion.10 = f32[40,7168]{1,0:T(8,128)} fusion(bf16[1,2,896,7168]{3,2,1,0:T(8,128)(2,1)} %param.13, f32[164,896]{1,0:T(8,128)S(1)} %convert_element_type.133, s32[]{:T(128)S(6)} %select_n.360, f32[40]{0:T(128)S(1)} %get-tuple-element.230, f32[896]{0:T(1024)S(1)} %fusion.139), kind=kOutput, calls=%fused_computation.14 | convolution fusion | flops 513909760 | bytes 14139908 | tf_op jit(solution)/shard_map/dot_general | solution.py:72
  107.8 8.3 %fusion.8 = f32[40,7168]{1,0:T(8,128)} fusion(bf16[1,2,896,7168]{3,2,1,0:T(8,128)(2,1)} %param.13, f32[164,896]{1,0:T(8,128)S(1)} %convert_element_type.133, s32[]{:T(128)S(6)} %select_n.367, f32[40]{0:T(128)S(1)} %get-tuple-element.229, f32[896]{0:T(1024)S(1)} %fusion.139), kind=kOutput, calls=%fused_computation.12 | convolution fusion | flops 513909760 | bytes 14139908 | tf_op jit(solution)/shard_map/dot_general | solution.py:72
  116.0 8.3 %fusion.6 = f32[40,7168]{1,0:T(8,128)} fusion(bf16[1,2,896,7168]{3,2,1,0:T(8,128)(2,1)} %param.13, f32[164,896]{1,0:T(8,128)} %copy-done.15, s32[]{:T(128)S(6)} %select_n.374, f32[40]{0:T(128)S(1)} %get-tuple-element.228, f32[896]{0:T(1024)S(1)} %fusion.139), kind=kOutput, calls=%fused_computation.10 | convolution fusion | flops 513909760 | bytes 14139044 | tf_op jit(solution)/shard_map/dot_general | solution.py:72
  124.4 8.1 %fusion.4 = f32[40,7168]{1,0:T(8,128)} fusion(bf16[1,2,896,7168]{3,2,1,0:T(8,128)(2,1)} %param.13, f32[164,896]{1,0:T(8,128)S(1)} %copy-done.16, s32[]{:T(128)S(6)} %select_n.381, f32[40]{0:T(128)S(1)} %get-tuple-element.227, f32[896]{0:T(1024)S(1)} %fusion.139), kind=kOutput, calls=%fused_computation.8 | convolution fusion | flops 513909760 | bytes 14139908 | tf_op jit(solution)/shard_map/dot_general | solution.py:72
  132.5 3.4 fusion.2
  136.0 3.4 fusion
  141.1 4.4 fusion.64
  145.5 57.9 %all-reduce.8 = bf16[40,7168]{1,0:T(8,128)(2,1)S(1)} all-reduce(f32[40,7168]{1,0:T(8,128)} %fusion.64), channel_id=1, replica_groups=mesh['segment'=4,'vocab'=8] {'vocab'}, use_global_device_ids=true, to_apply=%region_5.6 | all-reduce | flops 286720 | bytes 1720320 | tf_op jit(solution)/shard_map/psum | solution.py:82
  206.3 3.7 collective-permute-done.1
  210.0 8.0 %fusion.61 = f32[40,7168]{1,0:T(8,128)} fusion(f32[40,7168]{1,0:T(8,128)S(1)} %copy-done.6, f32[40,7168]{1,0:T(8,128)S(1)} %copy-done.14, bf16[40,896]{1,0:T(8,128)(2,1)S(1)} %collective-permute-done.1, bf16[1,2,896,7168]{3,2,1,0:T(8,128)(2,1)} %param.13, pred[]{:T(512)S(6)} %eq.30), kind=kOutput, calls=%fused_computation.43 | convolution fusion | flops 514375680 | bytes 16357377 | tf_op jit(solution)/shard_map/dot_general | solution.py:71
  218.1 59.6 %all-reduce.9 = bf16[40,7168]{1,0:T(8,128)(2,1)S(1)} all-reduce(f32[40,7168]{1,0:T(8,128)} %fusion.61), channel_id=1, replica_groups=mesh['segment'=4,'vocab'=8] {'vocab'}, use_global_device_ids=true, to_apply=%region_8.9 | all-reduce | flops 286720 | bytes 1720320 | tf_op jit(solution)/shard_map/psum | solution.py:82
  284.1 8.0 %fusion.58 = f32[40,7168]{1,0:T(8,128)} fusion(f32[40,7168]{1,0:T(8,128)} %convert_dynamic-update-slice_fusion.3, f32[40,7168]{1,0:T(8,128)S(1)} %copy-done.13, bf16[40,896]{1,0:T(8,128)(2,1)S(1)} %collective-permute-done.2, bf16[1,2,896,7168]{3,2,1,0:T(8,128)(2,1)} %param.13, pred[]{:T(512)S(6)} %eq.30), kind=kOutput, calls=%fused_computation.42 | convolution fusion | flops 514375680 | bytes 16357377 | tf_op jit(solution)/shard_map/dot_general | solution.py:71
  292.1 58.2 %all-reduce.10 = bf16[40,7168]{1,0:T(8,128)(2,1)S(1)} all-reduce(f32[40,7168]{1,0:T(8,128)} %fusion.58), channel_id=1, replica_groups=mesh['segment'=4,'vocab'=8] {'vocab'}, use_global_device_ids=true, to_apply=%region_11.12 | all-reduce | flops 286720 | bytes 1720320 | tf_op jit(solution)/shard_map/psum | solution.py:82
  353.0 3.9 collective-permute-done.3
  356.9 8.0 %fusion.55 = f32[40,7168]{1,0:T(8,128)} fusion(f32[40,7168]{1,0:T(8,128)S(1)} %copy-done.8, f32[40,7168]{1,0:T(8,128)S(1)} %copy-done.12, bf16[40,896]{1,0:T(8,128)(2,1)S(1)} %collective-permute-done.3, bf16[1,2,896,7168]{3,2,1,0:T(8,128)(2,1)} %param.13, pred[]{:T(512)S(6)} %eq.30), kind=kOutput, calls=%fused_computation.41 | convolution fusion | flops 514375680 | bytes 16357377 | tf_op jit(solution)/shard_map/dot_general | solution.py:71
  365.0 59.4 %all-reduce.11 = bf16[40,7168]{1,0:T(8,128)(2,1)S(1)} all-reduce(f32[40,7168]{1,0:T(8,128)} %fusion.55), channel_id=1, replica_groups=mesh['segment'=4,'vocab'=8] {'vocab'}, use_global_device_ids=true, to_apply=%region_14.15 | all-reduce | flops 286720 | bytes 1720320 | tf_op jit(solution)/shard_map/psum | solution.py:82
  426.8 4.0 collective-permute-done.4
  430.8 8.0 %fusion.52 = f32[40,7168]{1,0:T(8,128)} fusion(f32[40,7168]{1,0:T(8,128)} %convert_dynamic-update-slice_fusion.1, f32[40,7168]{1,0:T(8,128)S(1)} %copy-done.11, bf16[40,896]{1,0:T(8,128)(2,1)S(1)} %collective-permute-done.4, bf16[1,2,896,7168]{3,2,1,0:T(8,128)(2,1)} %param.13, pred[]{:T(512)S(6)} %eq.30), kind=kOutput, calls=%fused_computation.40 | convolution fusion | flops 514375680 | bytes 16357377 | tf_op jit(solution)/shard_map/dot_general | solution.py:71
  438.8 58.8 %all-reduce.12 = bf16[40,7168]{1,0:T(8,128)(2,1)} all-reduce(f32[40,7168]{1,0:T(8,128)} %fusion.52), channel_id=1, replica_groups=mesh['segment'=4,'vocab'=8] {'vocab'}, use_global_device_ids=true, to_apply=%region_17.18 | all-reduce | flops 286720 | bytes 1720320 | tf_op jit(solution)/shard_map/psum | solution.py:82
  501.6 3.5 collective-permute-done.5
  505.2 8.3 %fusion.49 = f32[40,7168]{1,0:T(8,128)} fusion(f32[40,7168]{1,0:T(8,128)S(1)} %copy-done.10, f32[40,7168]{1,0:T(8,128)} %fusion, bf16[40,896]{1,0:T(8,128)(2,1)S(1)} %collective-permute-done.5, bf16[1,2,896,7168]{3,2,1,0:T(8,128)(2,1)} %param.13, pred[]{:T(512)S(6)} %eq.30), kind=kOutput, calls=%fused_computation.39 | convolution fusion | flops 514375680 | bytes 16357377 | tf_op jit(solution)/shard_map/dot_general | solution.py:71
  513.5 59.9 %all-reduce.13 = bf16[40,7168]{1,0:T(8,128)(2,1)} all-reduce(f32[40,7168]{1,0:T(8,128)} %fusion.49), channel_id=1, replica_groups=mesh['segment'=4,'vocab'=8] {'vocab'}, use_global_device_ids=true, to_apply=%region_20.21 | all-reduce | flops 286720 | bytes 1720320 | tf_op jit(solution)/shard_map/psum | solution.py:82
  574.6 8.1 %fusion.172 = (f32[40]{0:T(128)S(1)}, f32[40,1024]{1,0:T(8,128)S(1)}) fusion(bf16[7168,1024]{1,0:T(8,128)(2,1)} %all-gather.5.cloned.1.call-done, f32[7168]{0:T(1024)S(1)} %bitcast.105, f32[40]{0:T(128)S(1)} %add_rsqrt_fusion.7, bf16[40,7168]{1,0:T(8,128)(2,1)S(1)} %all-reduce.7), kind=kOutput, calls=%fused_computation.245 | convolution fusion | flops 588390336 | bytes 15446336 | tf_op jit(solution)/shard_map/dot_general | solution.py:93
  593.8 2.9 fusion.177
  603.5 11.1 %all-gather.2 = f32[8,1,160]{2,1,0:T(1,128)S(1)} all-gather(f32[1,1,160]{2,1,0:T(1,128)S(1)} %select_n.451), channel_id=1, replica_groups=mesh['segment'=4,'vocab'=8] {'vocab'}, dimensions={0}, use_global_device_ids=true | all-gather | bytes 5760 | tf_op jit(solution)/shard_map/all_gather | solution.py:19
  615.5 9.6 %all-gather.1 = f32[8,1,160]{2,1,0:T(1,128)S(1)} all-gather(f32[1,1,160]{2,1,0:T(1,128)S(1)} %select_n.450), channel_id=1, replica_groups=mesh['segment'=4,'vocab'=8] {'vocab'}, dimensions={0}, use_global_device_ids=true | all-gather | bytes 5760 | tf_op jit(solution)/shard_map/all_gather | solution.py:19
  626.3 9.3 %all-gather = f32[8,1,160]{2,1,0:T(1,128)S(1)} all-gather(f32[1,1,160]{2,1,0:T(1,128)S(1)} %select_n.449), channel_id=1, replica_groups=mesh['segment'=4,'vocab'=8] {'vocab'}, dimensions={0}, use_global_device_ids=true | all-gather | bytes 5760 | tf_op jit(solution)/shard_map/all_gather | solution.py:19
  (192 shorter events, 48.0 us)
Async XLA Ops:
  6.5 568.1 %all-gather.5.cloned.1.call-start = ((), (), s32[]{:S(2)}) async-start(), calls=%async_computation | async-start | bytes 18350080 | tf_op jit(solution)/shard_map/all_gather | solution.py:57
  7.3 14.3 %copy-start.20 = (bf16[3,896]{1,0:T(4,128)(2,1)S(1)}, bf16[3,896]{1,0:T(4,128)(2,1)}, u32[]{:S(2)}) copy-start(bf16[3,896]{1,0:T(4,128)(2,1)} %param.15) | copy-start | bytes 16132
  7.7 100.1 %copy-start.15 = (f32[164,896]{1,0:T(8,128)}, f32[164,896]{1,0:T(8,128)S(1)}, u32[]{:S(2)}) copy-start(f32[164,896]{1,0:T(8,128)S(1)} %convert_element_type.133) | copy-start | bytes 1763332
  93.0 4.4 copy-start.19
  94.0 47.1 %collective-permute-start = (bf16[40,896]{1,0:T(8,128)(2,1)S(1)}, bf16[40,896]{1,0:T(8,128)(2,1)S(1)}, u32[]{:S(2)}, u32[]{:S(2)}) collective-permute-start(bf16[40,896]{1,0:T(8,128)(2,1)S(1)} %multiply_convert_fusion.23), channel_id=1, source_target_pairs={{0,8},{8,16},{16,24},{1,9},{9,17},{17,25},{2,10},{10,18},{18,26},{... | collective-permute-start | bytes 215048 | tf_op jit(solution)/shard_map/ppermute | solution.py:15
  99.6 32.9 %slice-start = ((s8[25690112]{0:T(1024)(128)(4,1)}), s8[4194304]{0:T(1024)(128)(4,1)S(1)}, s32[]{:S(2)}) async-start(s8[25690112]{0:T(1024)(128)(4,1)} %bitcast.103), calls=%async_computation.1 | async-start | bytes 8388608
  99.6 32.9 %slice-start.1 = ((s8[25690112]{0:T(1024)(128)(4,1)}), s8[4194304]{0:T(1024)(128)(4,1)S(1)}, s32[]{:S(2)}) async-start(s8[25690112]{0:T(1024)(128)(4,1)} %bitcast.103), calls=%async_computation.2 | async-start | bytes 8388608
  107.8 24.7 %slice-start.2 = ((s8[25690112]{0:T(1024)(128)(4,1)}), s8[4194304]{0:T(1024)(128)(4,1)S(1)}, s32[]{:S(2)}) async-start(s8[25690112]{0:T(1024)(128)(4,1)} %bitcast.103), calls=%async_computation.3 | async-start | bytes 8388608
  107.8 24.7 %slice-start.3 = ((s8[25690112]{0:T(1024)(128)(4,1)}), s8[4194304]{0:T(1024)(128)(4,1)S(1)}, s32[]{:S(2)}) async-start(s8[25690112]{0:T(1024)(128)(4,1)} %bitcast.103), calls=%async_computation.4 | async-start | bytes 8388608
  116.0 8.3 %copy-start.16 = (f32[164,896]{1,0:T(8,128)S(1)}, f32[164,896]{1,0:T(8,128)}, u32[]{:S(2)}) copy-start(f32[164,896]{1,0:T(8,128)} %copy-done.15) | copy-start | bytes 1763332
  116.0 16.5 %slice-start.4 = ((s8[25690112]{0:T(1024)(128)(4,1)}), s8[4194304]{0:T(1024)(128)(4,1)S(1)}, s32[]{:S(2)}) async-start(s8[25690112]{0:T(1024)(128)(4,1)} %bitcast.103), calls=%async_computation.5 | async-start | bytes 8388608
  116.0 16.5 %slice-start.5 = ((s8[25690112]{0:T(1024)(128)(4,1)}), s8[4194304]{0:T(1024)(128)(4,1)S(1)}, s32[]{:S(2)}) async-start(s8[25690112]{0:T(1024)(128)(4,1)} %bitcast.103), calls=%async_computation.6 | async-start | bytes 8388608
  124.3 8.2 %slice-start.6 = ((s8[25690112]{0:T(1024)(128)(4,1)}), s8[524288]{0:T(1024)(128)(4,1)S(1)}, s32[]{:S(2)}) async-start(s8[25690112]{0:T(1024)(128)(4,1)} %bitcast.103), calls=%async_computation.7 | async-start | bytes 1048576
  203.5 6.6 %copy-start.14 = (f32[40,7168]{1,0:T(8,128)S(1)}, f32[40,7168]{1,0:T(8,128)}, u32[]{:S(2)}) copy-start(f32[40,7168]{1,0:T(8,128)} %fusion.8) | copy-start | bytes 3440644
  203.5 6.5 %copy-start.6 = (f32[40,7168]{1,0:T(8,128)S(1)}, f32[40,7168]{1,0:T(8,128)}, u32[]{:S(2)}) copy-start(f32[40,7168]{1,0:T(8,128)} %copy-done.5) | copy-start | bytes 3440644
  203.9 6.1 collective-permute-start.1
  206.3 3.7 copy-start.7
  277.8 6.3 copy-start.13
  278.1 6.0 collective-permute-start.2
  350.4 6.6 %copy-start.12 = (f32[40,7168]{1,0:T(8,128)S(1)}, f32[40,7168]{1,0:T(8,128)}, u32[]{:S(2)}) copy-start(f32[40,7168]{1,0:T(8,128)} %fusion.4) | copy-start | bytes 3440644
  350.5 6.5 %copy-start.8 = (f32[40,7168]{1,0:T(8,128)S(1)}, f32[40,7168]{1,0:T(8,128)}, u32[]{:S(2)}) copy-start(f32[40,7168]{1,0:T(8,128)} %copy-done.7) | copy-start | bytes 3440644
  350.8 6.1 collective-permute-start.3
  353.0 3.9 copy-start.9
  424.3 2.4 copy-start.22
  424.3 6.4 copy-start.11
  424.8 6.0 collective-permute-start.4
  497.6 1.3 copy-start.1
  497.6 7.6 %copy-start.10 = (f32[40,7168]{1,0:T(8,128)S(1)}, f32[40,7168]{1,0:T(8,128)}, u32[]{:S(2)}) copy-start(f32[40,7168]{1,0:T(8,128)} %copy-done.9) | copy-start | bytes 3440644
  499.2 6.0 collective-permute-start.5
  574.6 9.3 %copy-start = (bf16[7168,1024]{1,0:T(8,128)(2,1)S(1)}, bf16[7168,1024]{1,0:T(8,128)(2,1)}, u32[]{:S(2)}) copy-start(bf16[7168,1024]{1,0:T(8,128)(2,1)} %all-gather.5.cloned.1.call-done) | copy-start | bytes 44040196
  590.1 3.6 copy-start.2
  596.6 3.5 copy-start.3
  (5 other events, 4.7 us)
Sparse Core Ops, SparseCore 0:
  9.2 141.4 all-gather.4
where the time goes:
time: 648 us; the launch traced here: 644 us
  blocking collectives  454 us (70%)
  matrix products  123 us (19%)
  waiting for transfers between devices  18.1 us (3%)
  between operations  14.3 us (2%)
  starting transfers between devices  13.8 us (2%)
  other arithmetic  11.7 us (2%)
  local copies, waits for them, and re-layouts  7.92 us (1%)
    psum x7, blocking collectives, per_device(): lax.psum(jnp.where(leading, placed, partial_value), 'vocab')  411 us
    dot_general x7, matrix products, per_device(): jnp.dot(incoming, module_block[0], preferred_element_type=jnp.float32)  50.8 us
    dot_general x7, matrix products, per_device(): jnp.dot(embed_normed, module_block[1], preferred_element_type=jnp.float32)  47.2 us
    all_gather x3, blocking collectives, combined_all(): everything = jax.tree.map(lambda part: lax.all_gather(part, axis), shard)  30.1 us
    dot_general x7, matrix products, per_device(): logits = jnp.dot(head_input, whole_head, preferred_element_type=jnp.float32)  25.3 us
    ppermute x6, waiting for transfers between devices, passed_along(): return lax.ppermute(block, axis, route)  17.4 us
    psum x1, blocking collectives, per_device(): lax.psum(jnp.sum(embed_float * embed_float, axis=1), 'vocab')  13.8 us
    ppermute x6, starting transfers between devices, passed_along(): return lax.ppermute(block, axis, route)  13.8 us
  transfers between devices with their start and end apart: 7, of which 5 were waited for; matrix products, arithmetic and copies ran while one was open for 17% of the time, Pallas kernels for 0%

commit v1 on v0

--- a/solution.py
+++ b/solution.py
@@ -79,9 +79,9 @@
             shard_index * local_width,
             1,
         )
-        full_rows = lax.psum(jnp.where(leading, placed, partial_value), "vocab").astype(
-            jnp.bfloat16
-        )
+        full_rows = jnp.sum(
+            lax.all_gather(jnp.where(leading, placed, partial_value), "vocab"), axis=0
+        ).astype(jnp.bfloat16)
         rows_float = full_rows.astype(jnp.float32)
         inverse_rms = lax.rsqrt(jnp.mean(rows_float * rows_float, axis=1, keepdims=True) + EPSILON)
         head_input = (rows_float * inverse_rms * out_scaling).astype(jnp.bfloat16)

time: 648 us -> 948 us (1.46)
  waiting for transfers between devices: 18.1 us -> 678 us
  blocking collectives: 454 us -> 41.9 us
  other arithmetic: 11.7 us -> 46.1 us
  matrix products: 123 us -> 134 us
    all_gather x0 -> x7, waiting for transfers between devices: none -> 546 us  [per_device(): lax.all_gather(jnp.where(leading, placed, partial_value), 'vocab')]
    psum x7 -> x0, blocking collectives: 411 us -> none  [per_device(): lax.psum(jnp.where(leading, placed, partial_value), 'vocab')]
    all_gather x1, waiting for transfers between devices: 0.02 us -> 118 us  [per_device(): whole_head = lax.all_gather(head_weight, 'segment', axis=0, tiled=True)]
    reduce_sum x0 -> x7, other arithmetic: none -> 29.4 us  [per_device(): jnp.sum(lax.all_gather(jnp.where(leading, placed, partial_value), 'vocab'...]
  transfers between devices with their start and end apart: 7 -> 14, of which waited for: 5 -> 14; matrix products, arithmetic and copies ran while one was open for 17% -> 9% of each run, Pallas kernels for 0% -> 0%
where the time goes in v1:
time: 948 us; the launch traced here: 939 us
  waiting for transfers between devices  678 us (72%)
  matrix products  134 us (14%)
  other arithmetic  46.1 us (5%)
  blocking collectives  41.9 us (4%)
  starting transfers between devices  19.7 us (2%)
  between operations  14.5 us (2%)
    all_gather x7, waiting for transfers between devices, per_device(): lax.all_gather(jnp.where(leading, placed, partial_value), 'vocab')  546 us
    all_gather x1, waiting for transfers between devices, per_device(): whole_head = lax.all_gather(head_weight, 'segment', axis=0, tiled=True)  118 us
    dot_general x7, matrix products, per_device(): jnp.dot(incoming, module_block[0], preferred_element_type=jnp.float32)  57.7 us
    dot_general x7, matrix products, per_device(): jnp.dot(embed_normed, module_block[1], preferred_element_type=jnp.float32)  46.3 us
    dot_general x7, matrix products, per_device(): logits = jnp.dot(head_input, whole_head, preferred_element_type=jnp.float32)  30.4 us
    reduce_sum x7, other arithmetic, per_device(): jnp.sum(lax.all_gather(jnp.where(leading, placed, partial_value), 'vocab'...  29.4 us
    all_gather x3, blocking collectives, combined_all(): everything = jax.tree.map(lambda part: lax.all_gather(part, axis), shard)  28.1 us
  transfers between devices with their start and end apart: 14, of which 14 were waited for; matrix products, arithmetic and copies ran while one was open for 9% of the time, Pallas kernels for 0%

profile of v1, /device:TPU:5, one launch (start us, length us, event | category | flops | bytes accessed | tf_op | source)
XLA Modules:
  0.0 938.7 jit_solution(6683939558734742536)
XLA Ops:
  8.9 13.8 %psum.7 = f32[164]{0:T(256)S(1)} all-reduce(f32[164]{0:T(256)S(1)} %multiply_reduce_fusion.6), channel_id=1, replica_groups=mesh['segment'=4,'vocab'=8] {'vocab'}, use_global_device_ids=true, to_apply=%region_1.0 | all-reduce | flops 164 | bytes 1312 | tf_op jit(solution)/shard_map/psum | solution.py:45
  23.9 5.9 fusion.12
  29.8 8.0 fusion.67
  38.5 6.0 fusion.10
  44.5 83.4 %all-gather.21.cloned.1.call-done = f32[320,7168]{1,0:T(8,128)} async-done(((f32[40,7168]{1,0:T(8,128)}), f32[320,7168]{1,0:T(8,128)}) %all-gather.21.cloned.1.call-update) | async-done | bytes 9175056 | tf_op jit(solution)/shard_map/all_gather | solution.py:83
  127.9 4.2 reduce_sum.262
  138.9 8.0 fusion.64
  146.9 6.0 fusion.8
  152.9 81.1 %all-gather.23.cloned.1.call-done = f32[320,7168]{1,0:T(8,128)} async-done(((f32[40,7168]{1,0:T(8,128)}), f32[320,7168]{1,0:T(8,128)}) %all-gather.23.cloned.1.call-update) | async-done | bytes 9175056 | tf_op jit(solution)/shard_map/all_gather | solution.py:83
  234.0 4.2 reduce_sum.264
  244.9 8.0 fusion.61
  253.6 6.0 fusion.6
  259.5 80.5 %all-gather.25.cloned.1.call-done = f32[320,7168]{1,0:T(8,128)} async-done(((f32[40,7168]{1,0:T(8,128)}), f32[320,7168]{1,0:T(8,128)}) %all-gather.25.cloned.1.call-update) | async-done | bytes 9175056 | tf_op jit(solution)/shard_map/all_gather | solution.py:83
  340.0 4.2 reduce_sum.266
  351.0 8.0 fusion.58
  359.1 6.0 fusion.4
  365.1 81.0 %all-gather.27.cloned.1.call-done = f32[320,7168]{1,0:T(8,128)} async-done(((f32[40,7168]{1,0:T(8,128)}), f32[320,7168]{1,0:T(8,128)}) %all-gather.27.cloned.1.call-update) | async-done | bytes 9175056 | tf_op jit(solution)/shard_map/all_gather | solution.py:83
  446.1 4.2 reduce_sum.268
  457.0 8.0 fusion.55
  465.1 8.2 fusion.2
  473.3 78.9 %all-gather.29.cloned.1.call-done = f32[320,7168]{1,0:T(8,128)} async-done(((f32[40,7168]{1,0:T(8,128)}), f32[320,7168]{1,0:T(8,128)}) %all-gather.29.cloned.1.call-update) | async-done | bytes 9175056 | tf_op jit(solution)/shard_map/all_gather | solution.py:83
  563.2 8.0 fusion.52
  572.0 8.3 fusion
  580.4 77.9 %all-gather.31.cloned.1.call-done = f32[320,7168]{1,0:T(8,128)} async-done(((f32[40,7168]{1,0:T(8,128)}), f32[320,7168]{1,0:T(8,128)}) %all-gather.31.cloned.1.call-update) | async-done | bytes 9175056 | tf_op jit(solution)/shard_map/all_gather | solution.py:83
  669.3 9.6 %fusion.49 = f32[40,7168]{1,0:T(8,128)} fusion(f32[40,7168]{1,0:T(8,128)S(1)} %convert_dynamic-update-slice_fusion, f32[40,7168]{1,0:T(8,128)S(1)} %copy-done.1, bf16[40,896]{1,0:T(8,128)(2,1)S(1)} %collective-permute-done.5, bf16[1,2,896,7168]{3,2,1,0:T(8,128)(2,1)} %param.13, pred[]{:T(512)S(6)} %eq.30), kind=kOutput, calls=%fused_computation.39 | convolution fusion | flops 514375680 | bytes 16357377 | tf_op jit(solution)/shard_map/dot_general | solution.py:71
  679.9 118.0 %all-gather.19.cloned.1.call-done = bf16[7168,1024]{1,0:T(8,128)(2,1)} async-done(((bf16[1792,1024]{1,0:T(8,128)(2,1)}), bf16[7168,1024]{1,0:T(8,128)(2,1)}) %all-gather.19.cloned.1.call-update) | async-done | bytes 14680080 | tf_op jit(solution)/shard_map/all_gather | solution.py:57
  797.9 8.1 fusion.172
  825.2 63.5 %all-gather.33.cloned.1.call-done = f32[320,7168]{1,0:T(8,128)} async-done(((f32[40,7168]{1,0:T(8,128)}), f32[320,7168]{1,0:T(8,128)}) %all-gather.33.cloned.1.call-update) | async-done | bytes 9175056 | tf_op jit(solution)/shard_map/all_gather | solution.py:83
  893.1 8.0 fusion.178
  901.4 9.2 all-gather.7
  911.1 9.7 %all-gather.8 = f32[8,1,160]{2,1,0:T(1,128)S(1)} all-gather(f32[1,1,160]{2,1,0:T(1,128)S(1)} %select_n.450), channel_id=1, replica_groups=mesh['segment'=4,'vocab'=8] {'vocab'}, dimensions={0}, use_global_device_ids=true | all-gather | bytes 5760 | tf_op jit(solution)/shard_map/all_gather | solution.py:19
  921.1 9.1 all-gather.9
  (168 shorter events, 81.5 us)
Async XLA Ops:
  6.5 16.2 %copy-start.5 = (bf16[3,896]{1,0:T(4,128)(2,1)S(1)}, bf16[3,896]{1,0:T(4,128)(2,1)}, u32[]{:S(2)}) copy-start(bf16[3,896]{1,0:T(4,128)(2,1)} %param.15) | copy-start | bytes 16132
  6.5 121.4 %all-gather.21.cloned.1.call-start = ((), (), s32[]{:S(2)}) async-start(), calls=%async_computation.1 | async-start | bytes 10321920 | tf_op jit(solution)/shard_map/all_gather | solution.py:83
  7.6 246.0 %copy-start.3 = (f32[164,896]{1,0:T(8,128)}, f32[164,896]{1,0:T(8,128)S(1)}, u32[]{:S(2)}) copy-start(f32[164,896]{1,0:T(8,128)S(1)} %convert_element_type.133) | copy-start | bytes 1763332
  37.8 0.7 copy-start.6
  37.8 196.2 %all-gather.23.cloned.1.call-start = ((), (), s32[]{:S(2)}) async-start(), calls=%async_computation.2 | async-start | bytes 10321920 | tf_op jit(solution)/shard_map/all_gather | solution.py:83
  132.5 6.3 collective-permute-start
  146.9 193.2 %all-gather.25.cloned.1.call-start = ((), (), s32[]{:S(2)}) async-start(), calls=%async_computation.3 | async-start | bytes 10321920 | tf_op jit(solution)/shard_map/all_gather | solution.py:83
  238.6 6.3 collective-permute-start.1
  253.0 193.1 %all-gather.27.cloned.1.call-start = ((), (), s32[]{:S(2)}) async-start(), calls=%async_computation.4 | async-start | bytes 10321920 | tf_op jit(solution)/shard_map/all_gather | solution.py:83
  344.7 6.3 collective-permute-start.2
  359.0 193.1 %all-gather.29.cloned.1.call-start = ((), (), s32[]{:S(2)}) async-start(), calls=%async_computation.5 | async-start | bytes 10321920 | tf_op jit(solution)/shard_map/all_gather | solution.py:83
  450.7 6.3 collective-permute-start.3
  465.1 193.3 %all-gather.31.cloned.1.call-start = ((), (), s32[]{:S(2)}) async-start(), calls=%async_computation.6 | async-start | bytes 10321920 | tf_op jit(solution)/shard_map/all_gather | solution.py:83
  556.7 6.6 copy-start.2
  556.8 6.4 collective-permute-start.4
  571.2 226.6 %all-gather.19.cloned.1.call-start = ((), (), s32[]{:S(2)}) async-start(), calls=%async_computation | async-start | bytes 18350080 | tf_op jit(solution)/shard_map/all_gather | solution.py:57
  572.0 316.7 %all-gather.33.cloned.1.call-start = ((), (), s32[]{:S(2)}) async-start(), calls=%async_computation.7 | async-start | bytes 10321920 | tf_op jit(solution)/shard_map/all_gather | solution.py:83
  662.6 6.7 copy-start.1
  663.0 6.3 collective-permute-start.5
  678.9 0.7 copy-start.4
  678.9 0.8 copy-start.7
  797.9 9.5 %copy-start = (bf16[7168,1024]{1,0:T(8,128)(2,1)S(1)}, bf16[7168,1024]{1,0:T(8,128)(2,1)}, u32[]{:S(2)}) copy-start(bf16[7168,1024]{1,0:T(8,128)(2,1)} %all-gather.19.cloned.1.call-done) | copy-start | bytes 44040196
Sparse Core Ops, SparseCore 0:
  38.0 89.9 all-gather.20
  147.0 86.9 all-gather.22
  253.1 86.9 all-gather.24
  359.1 86.9 all-gather.26
  465.2 86.9 all-gather.28
  571.4 86.9 all-gather.30
  660.2 137.6 all-gather.18
  799.5 89.1 all-gather.32
